TPU v7x, 256 devices: a whole 4x4x8 slice. The times are simulated.
256 devices in a mesh: row: 16 (over y, z_lo, core), col: 16 (over z_hi, x).
Axes of the slice: x: 4, y: 4, z: 8 (z_hi: 4, z_lo: 2; z = z_hi * 2 + z_lo), core: 2. Of those that a mesh axis runs over, the one named last changes fastest.
Arguments:
- features: bfloat16 [131072, 256], P(('row', 'col')), may hold values from -6 to 6
- w_self: bfloat16 [256, 256], replicated, may hold values from -0.375 to 0.375
- w_neigh: bfloat16 [256, 256], replicated, may hold values from -3 to 3
- cotangent: bfloat16 [131072, 256], P(('row', 'col')), may hold values from -6 to 6
- degree: int32 [131072], P(('row', 'col')), may hold values from 64 to 256
- tile_rows: int32 [65536], P(('row', 'col')), may hold values from 0 to 63
- tile_cols: int32 [65536], P(('row', 'col')), may hold values from 0 to 63
- tile_edges: int32 [4, 65536, 128], P(None, ('row', 'col')), may hold values from 0 to 127
- tile_count: int32 [256], P(('row', 'col')), may hold values from 4 to 256, as said below
Outputs:
- activations: bfloat16 [131072, 256], P(('row', 'col'))
- feature_grad: bfloat16 [131072, 256], P(('row', 'col'))
- grad_self: float32 [256, 256], replicated
- grad_neigh: float32 [256, 256], replicated
Inputs may be any that keep to these rules, and one draw needn't show every extreme that they name: The busiest device uses all 256 of its slots; slots from tile_count on are ignored.
All inputs are finite; a program needn't handle non-finite values.
Results may differ from a plain program's by a relative error of at most 0.0059.
Values may be sent and summed in bfloat16 or wider, within the bound.
No kernel may reach another device: no remote copies, remote signals or barrier semaphores. Data moves between devices by JAX's collectives and lax.ppermute only.
A program may use at most 64 MiB of HBM per device.

v0:
```python
import math
import jax
import jax.numpy as jnp
from jax import lax
from jax.sharding import PartitionSpec as P


def tile_masks(edges_here, use_here):
    tile_size = edges_here.shape[2]
    matches = edges_here[:, :, :, None] == jnp.arange(tile_size, dtype=jnp.int32)
    multiplicity = jnp.sum(matches.astype(jnp.float32), axis=0)
    return (multiplicity * use_here[:, None, None]).astype(jnp.bfloat16)


def sum_weights(part_self, part_neigh):
    return lax.psum((part_self, part_neigh), ("row", "col"))


def spread_back(dscaled, row_blocks, col_blocks, edge_blocks, use_blocks, col_tile_count):
    tile_size = edge_blocks.shape[3]
    feature_dim = dscaled.shape[1]
    row_nodes = lax.all_gather(dscaled, "col", axis=0, tiled=True)
    row_tiles = row_nodes.reshape(-1, tile_size, feature_dim)

    def backward_round(running, inputs):
        rows_here, cols_here, edges_here, use_here = inputs
        pattern = tile_masks(edges_here, use_here)
        contribution = jnp.einsum(
            "bqc,bqf->bcf", pattern, row_tiles[rows_here], preferred_element_type=jnp.float32
        )
        return (running.at[cols_here].add(contribution), None)

    start_value = jnp.zeros((col_tile_count, tile_size, feature_dim), jnp.float32)
    partial_grads, _ = lax.scan(
        backward_round, start_value, (row_blocks, col_blocks, edge_blocks, use_blocks)
    )
    return lax.psum_scatter(
        partial_grads.reshape(-1, feature_dim), "row", scatter_dimension=0, tiled=True
    )


def per_device(
    features, w_self, w_neigh, cotangent, degree, tile_rows, tile_cols, tile_edges, tile_count
):
    local_rows, feature_dim = features.shape
    tile_size = tile_edges.shape[2]
    slot_count = tile_rows.shape[0]
    row_devices = lax.axis_size("row")
    col_devices = lax.axis_size("col")
    in_use = (jnp.arange(slot_count, dtype=jnp.int32) < tile_count[0]).astype(jnp.float32)
    block_size = math.gcd(slot_count, 32)
    rounds = slot_count // block_size
    edge_blocks = tile_edges.reshape(tile_edges.shape[0], rounds, block_size, tile_size).transpose(
        1, 0, 2, 3
    )
    row_blocks = tile_rows.reshape(rounds, block_size)
    col_blocks = tile_cols.reshape(rounds, block_size)
    use_blocks = in_use.reshape(rounds, block_size)
    row_tile_count = local_rows * col_devices // tile_size
    col_tile_count = local_rows * row_devices // tile_size
    column_nodes = lax.all_gather(features, "row", axis=0, tiled=True)
    column_tiles = column_nodes.reshape(-1, tile_size, feature_dim)

    def forward_round(running, inputs):
        rows_here, cols_here, edges_here, use_here = inputs
        pattern = tile_masks(edges_here, use_here)
        product = jnp.einsum(
            "bqc,bcf->bqf", pattern, column_tiles[cols_here], preferred_element_type=jnp.float32
        )
        return (running.at[rows_here].add(product), None)

    start_value = jnp.zeros((row_tile_count, tile_size, feature_dim), jnp.float32)
    partial_sums, _ = lax.scan(
        forward_round, start_value, (row_blocks, col_blocks, edge_blocks, use_blocks)
    )
    neighbour_sum = lax.psum_scatter(
        partial_sums.reshape(-1, feature_dim), "col", scatter_dimension=0, tiled=True
    )
    degree_wide = degree.astype(jnp.float32)[:, None]
    aggregate = (neighbour_sum / degree_wide).astype(jnp.bfloat16)
    preact = jnp.dot(features, w_self, preferred_element_type=jnp.float32) + jnp.dot(
        aggregate, w_neigh, preferred_element_type=jnp.float32
    )
    sigmoid_pre = jax.nn.sigmoid(preact)
    activations = (preact * sigmoid_pre).astype(jnp.bfloat16)
    slope = sigmoid_pre * (1.0 + preact * (1.0 - sigmoid_pre))
    dpreact = (cotangent.astype(jnp.float32) * slope).astype(jnp.bfloat16)
    part_self = jnp.einsum("nf,ng->fg", features, dpreact, preferred_element_type=jnp.float32)
    part_neigh = jnp.einsum("nf,ng->fg", aggregate, dpreact, preferred_element_type=jnp.float32)
    dscaled = (
        jnp.einsum("ng,fg->nf", dpreact, w_neigh, preferred_element_type=jnp.float32) / degree_wide
    ).astype(jnp.bfloat16)
    neighbour_grad = spread_back(
        dscaled, row_blocks, col_blocks, edge_blocks, use_blocks, col_tile_count
    )
    grad_pair = sum_weights(part_self, part_neigh)
    own_grad = jnp.einsum("ng,fg->nf", dpreact, w_self, preferred_element_type=jnp.float32)
    feature_grad = (own_grad + neighbour_grad).astype(jnp.bfloat16)
    total_nodes = local_rows * row_devices * col_devices
    grad_scale = 1.0 / math.sqrt(total_nodes)
    return (activations, feature_grad, grad_pair[0] * grad_scale, grad_pair[1] * grad_scale)


def solution(mesh):
    return jax.shard_map(
        per_device,
        mesh=mesh,
        in_specs=(
            P(("row", "col"), None),
            P(),
            P(),
            P(("row", "col"), None),
            P(("row", "col")),
            P(("row", "col")),
            P(("row", "col")),
            P(None, ("row", "col"), None),
            P(("row", "col")),
        ),
        out_specs=(P(("row", "col"), None), P(("row", "col"), None), P(), P()),
        check_vma=False,
    )
```

profile of v0, /device:TPU:2, one launch (start us, length us, event | category | flops | bytes accessed | tf_op | source)
XLA Modules:
  0.0 771.7 jit_solution(11886097251280555593)
XLA Ops:
  11.2 41.7 %all-gather.3.cloned.1.call-done = bf16[8192,256]{1,0:T(8,128)(2,1)} async-done(((bf16[512,256]{1,0:T(8,128)(2,1)}), bf16[8192,256]{1,0:T(8,128)(2,1)}) %all-gather.3.cloned.1.call-update) | async-done | bytes 4194320 | tf_op jit(solution)/shard_map/all_gather | solution.py:61
  52.9 4.3 broadcast.81.clone
  57.1 147.1 %while.20 = (s32[]{:T(128)}, f32[64,128,256]{2,1,0:T(8,128)}, s32[8,32]{1,0:T(8,128)S(1)}, s32[8,4,32,128]{3,2,1,0:T(8,128)S(1)}, f32[8,32]{1,0:T(8,128)S(1)}, /...) while((s32[]{:T(128)}, f32[64,128,256]{2,1,0:T(8,128)}, s32[8,32]{1,0:T(8,128)S(1)}, ...), condition=%wide.region_3.4_spmd, body=%wide.region_0.3_spmd.sunk | while | flops 276300992 | bytes 27465064 | solution.py:73
  65.7 9.8 %scatter_fusion = f32[64,128,256]{2,1,0:T(8,128)} fusion(f32[64,128,256]{2,1,0:T(8,128)} %get-tuple-element.261, s32[32]{0:T(128)S(1)} %get-tuple-element.241, f32[32,128,256]{2,1,0:T(8,128)} %fusion.44), kind=kCustom, calls=%fused_computation.2.clone.1 | custom fusion | flops 1048576 | bytes 12583040 | tf_op jit(solution)/shard_map/while/body/eval_jaxpr/scatter-add | solution.py:70
  84.2 9.7 %scatter_fusion = f32[64,128,256]{2,1,0:T(8,128)} fusion(f32[64,128,256]{2,1,0:T(8,128)} %get-tuple-element.261, s32[32]{0:T(128)S(1)} %get-tuple-element.241, f32[32,128,256]{2,1,0:T(8,128)} %fusion.44), kind=kCustom, calls=%fused_computation.2.clone.1 | custom fusion | flops 1048576 | bytes 12583040 | tf_op jit(solution)/shard_map/while/body/eval_jaxpr/scatter-add | solution.py:70
  102.4 9.7 %scatter_fusion = f32[64,128,256]{2,1,0:T(8,128)} fusion(f32[64,128,256]{2,1,0:T(8,128)} %get-tuple-element.261, s32[32]{0:T(128)S(1)} %get-tuple-element.241, f32[32,128,256]{2,1,0:T(8,128)} %fusion.44), kind=kCustom, calls=%fused_computation.2.clone.1 | custom fusion | flops 1048576 | bytes 12583040 | tf_op jit(solution)/shard_map/while/body/eval_jaxpr/scatter-add | solution.py:70
  120.7 9.6 %scatter_fusion = f32[64,128,256]{2,1,0:T(8,128)} fusion(f32[64,128,256]{2,1,0:T(8,128)} %get-tuple-element.261, s32[32]{0:T(128)S(1)} %get-tuple-element.241, f32[32,128,256]{2,1,0:T(8,128)} %fusion.44), kind=kCustom, calls=%fused_computation.2.clone.1 | custom fusion | flops 1048576 | bytes 12583040 | tf_op jit(solution)/shard_map/while/body/eval_jaxpr/scatter-add | solution.py:70
  139.0 9.8 %scatter_fusion = f32[64,128,256]{2,1,0:T(8,128)} fusion(f32[64,128,256]{2,1,0:T(8,128)} %get-tuple-element.261, s32[32]{0:T(128)S(1)} %get-tuple-element.241, f32[32,128,256]{2,1,0:T(8,128)} %fusion.44), kind=kCustom, calls=%fused_computation.2.clone.1 | custom fusion | flops 1048576 | bytes 12583040 | tf_op jit(solution)/shard_map/while/body/eval_jaxpr/scatter-add | solution.py:70
  157.3 9.8 %scatter_fusion = f32[64,128,256]{2,1,0:T(8,128)} fusion(f32[64,128,256]{2,1,0:T(8,128)} %get-tuple-element.261, s32[32]{0:T(128)S(1)} %get-tuple-element.241, f32[32,128,256]{2,1,0:T(8,128)} %fusion.44), kind=kCustom, calls=%fused_computation.2.clone.1 | custom fusion | flops 1048576 | bytes 12583040 | tf_op jit(solution)/shard_map/while/body/eval_jaxpr/scatter-add | solution.py:70
  175.7 9.9 %scatter_fusion = f32[64,128,256]{2,1,0:T(8,128)} fusion(f32[64,128,256]{2,1,0:T(8,128)} %get-tuple-element.261, s32[32]{0:T(128)S(1)} %get-tuple-element.241, f32[32,128,256]{2,1,0:T(8,128)} %fusion.44), kind=kCustom, calls=%fused_computation.2.clone.1 | custom fusion | flops 1048576 | bytes 12583040 | tf_op jit(solution)/shard_map/while/body/eval_jaxpr/scatter-add | solution.py:70
  194.2 10.0 %scatter_fusion = f32[64,128,256]{2,1,0:T(8,128)} fusion(f32[64,128,256]{2,1,0:T(8,128)} %get-tuple-element.261, s32[32]{0:T(128)S(1)} %get-tuple-element.241, f32[32,128,256]{2,1,0:T(8,128)} %fusion.44), kind=kCustom, calls=%fused_computation.2.clone.1 | custom fusion | flops 1048576 | bytes 12583040 | tf_op jit(solution)/shard_map/while/body/eval_jaxpr/scatter-add | solution.py:70
  205.4 119.9 %reduce-scatter.3.cloned.1.call-done = f32[512,256]{1,0:T(8,128)} async-done(((f32[8192,256]{1,0:T(8,128)}), f32[512,256]{1,0:T(8,128)}) %reduce-scatter.3.cloned.1.call-update) | async-done | bytes 524304 | tf_op jit(solution)/shard_map/reduce_scatter | solution.py:76
  330.7 72.7 %all-gather.5.cloned.1.call-done = bf16[8192,256]{1,0:T(8,128)(2,1)} async-done(((bf16[512,256]{1,0:T(8,128)(2,1)}), bf16[8192,256]{1,0:T(8,128)(2,1)}) %all-gather.5.cloned.1.call-update) | async-done | bytes 4194320 | tf_op jit(solution)/shard_map/all_gather | solution.py:22
  407.6 150.2 %while.21 = (s32[]{:T(128)}, f32[64,128,256]{2,1,0:T(8,128)}, s32[8,32]{1,0:T(8,128)S(1)}, s32[8,4,32,128]{3,2,1,0:T(8,128)S(1)}, f32[8,32]{1,0:T(8,128)S(1)}, /...) while((s32[]{:T(128)}, f32[64,128,256]{2,1,0:T(8,128)}, s32[8,32]{1,0:T(8,128)S(1)}, ...), condition=%wide.region_8.9_spmd, body=%wide.region_5.8_spmd.sunk | while | flops 276300992 | bytes 27465064 | solution.py:34
  416.4 9.9 %scatter_fusion.1 = f32[64,128,256]{2,1,0:T(8,128)} fusion(f32[64,128,256]{2,1,0:T(8,128)} %get-tuple-element.285, s32[32]{0:T(128)S(1)} %get-tuple-element.250, f32[32,128,256]{2,1,0:T(8,128)} %fusion.48), kind=kCustom, calls=%fused_computation.3.clone.1 | custom fusion | flops 1048576 | bytes 12583040 | tf_op jit(solution)/shard_map/while/body/eval_jaxpr/scatter-add | solution.py:31
  435.1 10.1 %scatter_fusion.1 = f32[64,128,256]{2,1,0:T(8,128)} fusion(f32[64,128,256]{2,1,0:T(8,128)} %get-tuple-element.285, s32[32]{0:T(128)S(1)} %get-tuple-element.250, f32[32,128,256]{2,1,0:T(8,128)} %fusion.48), kind=kCustom, calls=%fused_computation.3.clone.1 | custom fusion | flops 1048576 | bytes 12583040 | tf_op jit(solution)/shard_map/while/body/eval_jaxpr/scatter-add | solution.py:31
  453.9 10.0 %scatter_fusion.1 = f32[64,128,256]{2,1,0:T(8,128)} fusion(f32[64,128,256]{2,1,0:T(8,128)} %get-tuple-element.285, s32[32]{0:T(128)S(1)} %get-tuple-element.250, f32[32,128,256]{2,1,0:T(8,128)} %fusion.48), kind=kCustom, calls=%fused_computation.3.clone.1 | custom fusion | flops 1048576 | bytes 12583040 | tf_op jit(solution)/shard_map/while/body/eval_jaxpr/scatter-add | solution.py:31
  472.7 10.0 %scatter_fusion.1 = f32[64,128,256]{2,1,0:T(8,128)} fusion(f32[64,128,256]{2,1,0:T(8,128)} %get-tuple-element.285, s32[32]{0:T(128)S(1)} %get-tuple-element.250, f32[32,128,256]{2,1,0:T(8,128)} %fusion.48), kind=kCustom, calls=%fused_computation.3.clone.1 | custom fusion | flops 1048576 | bytes 12583040 | tf_op jit(solution)/shard_map/while/body/eval_jaxpr/scatter-add | solution.py:31
  491.5 10.1 %scatter_fusion.1 = f32[64,128,256]{2,1,0:T(8,128)} fusion(f32[64,128,256]{2,1,0:T(8,128)} %get-tuple-element.285, s32[32]{0:T(128)S(1)} %get-tuple-element.250, f32[32,128,256]{2,1,0:T(8,128)} %fusion.48), kind=kCustom, calls=%fused_computation.3.clone.1 | custom fusion | flops 1048576 | bytes 12583040 | tf_op jit(solution)/shard_map/while/body/eval_jaxpr/scatter-add | solution.py:31
  510.4 10.1 %scatter_fusion.1 = f32[64,128,256]{2,1,0:T(8,128)} fusion(f32[64,128,256]{2,1,0:T(8,128)} %get-tuple-element.285, s32[32]{0:T(128)S(1)} %get-tuple-element.250, f32[32,128,256]{2,1,0:T(8,128)} %fusion.48), kind=kCustom, calls=%fused_computation.3.clone.1 | custom fusion | flops 1048576 | bytes 12583040 | tf_op jit(solution)/shard_map/while/body/eval_jaxpr/scatter-add | solution.py:31
  529.2 9.9 %scatter_fusion.1 = f32[64,128,256]{2,1,0:T(8,128)} fusion(f32[64,128,256]{2,1,0:T(8,128)} %get-tuple-element.285, s32[32]{0:T(128)S(1)} %get-tuple-element.250, f32[32,128,256]{2,1,0:T(8,128)} %fusion.48), kind=kCustom, calls=%fused_computation.3.clone.1 | custom fusion | flops 1048576 | bytes 12583040 | tf_op jit(solution)/shard_map/while/body/eval_jaxpr/scatter-add | solution.py:31
  547.9 10.0 %scatter_fusion.1 = f32[64,128,256]{2,1,0:T(8,128)} fusion(f32[64,128,256]{2,1,0:T(8,128)} %get-tuple-element.285, s32[32]{0:T(128)S(1)} %get-tuple-element.250, f32[32,128,256]{2,1,0:T(8,128)} %fusion.48), kind=kCustom, calls=%fused_computation.3.clone.1 | custom fusion | flops 1048576 | bytes 12583040 | tf_op jit(solution)/shard_map/while/body/eval_jaxpr/scatter-add | solution.py:31
  557.9 103.7 %all-reduce.3.cloned.1.call-done = (f32[256,256]{0,1:T(8,128)}, f32[256,256]{0,1:T(8,128)}) async-done(((f32[256,256]{0,1:T(8,128)}, f32[256,256]{0,1:T(8,128)}), (f32[256,256]{0,1:T(8,128)}, f32[256,256]{0,1:T(8,128)})) %all-reduce.3.cloned.1.call-update) | async-done | bytes 524304 | tf_op jit(solution)/shard_map/psum | solution.py:16
  664.4 98.7 %reduce-scatter.5.cloned.1.call-done = f32[512,256]{1,0:T(8,128)} async-done(((f32[8192,256]{1,0:T(8,128)}), f32[512,256]{1,0:T(8,128)}) %reduce-scatter.5.cloned.1.call-update) | async-done | bytes 524304 | tf_op jit(solution)/shard_map/reduce_scatter | solution.py:37
  (148 shorter events, 157.3 us)
Async XLA Ops:
  7.2 319.3 %copy-start = (bf16[256,256]{1,0:T(8,128)(2,1)S(1)}, bf16[256,256]{1,0:T(8,128)(2,1)}, u32[]{:S(2)}) copy-start(bf16[256,256]{1,0:T(8,128)(2,1)} %param.15) | copy-start | bytes 393220
  7.2 45.7 %all-gather.3.cloned.1.call-start = ((), (), s32[]{:S(2)}) async-start(), calls=%async_computation.2 | async-start | bytes 4456448 | tf_op jit(solution)/shard_map/all_gather | solution.py:61
  7.9 317.4 %reduce-scatter.3.cloned.1.call-start = ((), (), s32[]{:S(2)}) async-start(), calls=%async_computation.3 | async-start | bytes 8912896 | tf_op jit(solution)/shard_map/reduce_scatter | solution.py:76
  204.2 0.7 copy-start.3
  204.2 1.0 copy-start.1
  204.2 1.0 copy-start.2
  204.2 122.3 %copy-start.4 = (bf16[512,256]{1,0:T(8,128)(2,1)S(1)}, bf16[512,256]{1,0:T(8,128)(2,1)}, u32[]{:S(2)}) copy-start(bf16[512,256]{1,0:T(8,128)(2,1)} %param.16) | copy-start | bytes 786436
  204.2 199.1 %all-gather.5.cloned.1.call-start = ((), (), s32[]{:S(2)}) async-start(), calls=%async_computation.4 | async-start | bytes 4456448 | tf_op jit(solution)/shard_map/all_gather | solution.py:22
  328.6 333.0 %all-reduce.3.cloned.1.call-start = ((), (), s32[]{:S(2)}) async-start(), calls=%async_computation.6 | async-start | bytes 1048576 | tf_op jit(solution)/shard_map/psum | solution.py:16
  330.6 432.5 %reduce-scatter.5.cloned.1.call-start = ((), (), s32[]{:S(2)}) async-start(), calls=%async_computation.5 | async-start | bytes 8912896 | tf_op jit(solution)/shard_map/reduce_scatter | solution.py:37
Sparse Core Ops, SparseCore 0:
  9.9 42.9 all-gather.2
  204.4 120.8 reduce-scatter.2
  328.7 74.6 all-gather.4
  409.4 252.1 all-reduce.2
  664.0 99.0 reduce-scatter.4
where the time goes:
time: 773 us; the launch traced here: 772 us
  waiting for transfers between devices  437 us (57%)
  other arithmetic  208 us (27%)
  local copies, waits for them, and re-layouts  60 us (8%)
  matrix products  51.1 us (7%)
  between operations  14.5 us (2%)
    reduce_scatter x1, waiting for transfers between devices, per_device(): lax.psum_scatter(partial_sums.reshape(-1, feature_dim), 'col', scatter_di...  120 us
    psum x1, waiting for transfers between devices, sum_weights(): return lax.psum((part_self, part_neigh), ('row', 'col'))  104 us
    reduce_scatter x1, waiting for transfers between devices, spread_back(): lax.psum_scatter(partial_grads.reshape(-1, feature_dim), 'row', scatter_d...  98.7 us
    scatter-add x8, other arithmetic, backward_round(): return (running.at[cols_here].add(contribution), None)  80.1 us
    scatter-add x8, other arithmetic, forward_round(): return (running.at[rows_here].add(product), None)  78.3 us
    all_gather x1, waiting for transfers between devices, spread_back(): row_nodes = lax.all_gather(dscaled, 'col', axis=0, tiled=True)  72.7 us
    reduce_sum x16, other arithmetic, tile_masks(): multiplicity = jnp.sum(matches.astype(jnp.float32), axis=0)  46.9 us
    all_gather x1, waiting for transfers between devices, per_device(): column_nodes = lax.all_gather(features, 'row', axis=0, tiled=True)  41.7 us
  transfers between devices with their start and end apart: 5, of which 5 were waited for; matrix products, arithmetic and copies ran while one was open for 21% of the time, Pallas kernels for 0%

commit v1 on v0

--- a/solution.py
+++ b/solution.py
@@ -13,7 +13,7 @@
 
 
 def sum_weights(part_self, part_neigh):
-    return lax.psum((part_self, part_neigh), ("row", "col"))
+    return lax.psum(lax.psum((part_self, part_neigh), "row"), "col")
 
 
 def spread_back(dscaled, row_blocks, col_blocks, edge_blocks, use_blocks, col_tile_count):

time: 773 us -> 810 us (1.048)
  waiting for transfers between devices: 437 us -> 475 us
    psum x1 -> x2, waiting for transfers between devices: 104 us -> 134 us  [sum_weights(): return lax.psum(lax.psum((part_self, part_neigh), 'row'), 'col')]
  transfers between devices with their start and end apart: 5 -> 6, of which waited for: 5 -> 6; matrix products, arithmetic and copies ran while one was open for 21% -> 20% of each run, Pallas kernels for 0% -> 0%
where the time goes in v1:
time: 810 us; the launch traced here: 809 us
  waiting for transfers between devices  475 us (59%)
  other arithmetic  208 us (26%)
  local copies, waits for them, and re-layouts  60 us (7%)
  matrix products  51 us (6%)
  between operations  14.8 us (2%)
    psum x2, waiting for transfers between devices, sum_weights(): return lax.psum(lax.psum((part_self, part_neigh), 'row'), 'col')  134 us
    reduce_scatter x1, waiting for transfers between devices, per_device(): lax.psum_scatter(partial_sums.reshape(-1, feature_dim), 'col', scatter_di...  120 us
    reduce_scatter x1, waiting for transfers between devices, spread_back(): lax.psum_scatter(partial_grads.reshape(-1, feature_dim), 'row', scatter_d...  99 us
    scatter-add x8, other arithmetic, backward_round(): return (running.at[cols_here].add(contribution), None)  80.1 us
    all_gather x1, waiting for transfers between devices, spread_back(): row_nodes = lax.all_gather(dscaled, 'col', axis=0, tiled=True)  79.2 us
    scatter-add x8, other arithmetic, forward_round(): return (running.at[rows_here].add(product), None)  78.2 us
    reduce_sum x16, other arithmetic, tile_masks(): multiplicity = jnp.sum(matches.astype(jnp.float32), axis=0)  46.9 us
    all_gather x1, waiting for transfers between devices, per_device(): column_nodes = lax.all_gather(features, 'row', axis=0, tiled=True)  41.7 us
  transfers between devices with their start and end apart: 6, of which 6 were waited for; matrix products, arithmetic and copies ran while one was open for 20% of the time, Pallas kernels for 0%

profile of v1, /device:TPU:2, one launch (start us, length us, event | category | flops | bytes accessed | tf_op | source)
XLA Modules:
  0.0 809.0 jit_solution(18381005559218769921)
XLA Ops:
  11.2 41.7 %all-gather.3.cloned.1.call-done = bf16[8192,256]{1,0:T(8,128)(2,1)} async-done(((bf16[512,256]{1,0:T(8,128)(2,1)}), bf16[8192,256]{1,0:T(8,128)(2,1)}) %all-gather.3.cloned.1.call-update) | async-done | bytes 4194320 | tf_op jit(solution)/shard_map/all_gather | solution.py:61
  57.1 146.8 %while.20 = (s32[]{:T(128)}, f32[64,128,256]{2,1,0:T(8,128)}, s32[8,32]{1,0:T(8,128)S(1)}, s32[8,4,32,128]{3,2,1,0:T(8,128)S(1)}, f32[8,32]{1,0:T(8,128)S(1)}, /...) while((s32[]{:T(128)}, f32[64,128,256]{2,1,0:T(8,128)}, s32[8,32]{1,0:T(8,128)S(1)}, ...), condition=%wide.region_3.4_spmd, body=%wide.region_0.3_spmd.sunk | while | flops 276300992 | bytes 27465064 | solution.py:73
  65.7 9.8 %scatter_fusion = f32[64,128,256]{2,1,0:T(8,128)} fusion(f32[64,128,256]{2,1,0:T(8,128)} %get-tuple-element.263, s32[32]{0:T(128)S(1)} %get-tuple-element.243, f32[32,128,256]{2,1,0:T(8,128)} %fusion.44), kind=kCustom, calls=%fused_computation.2.clone.1 | custom fusion | flops 1048576 | bytes 12583040 | tf_op jit(solution)/shard_map/while/body/eval_jaxpr/scatter-add | solution.py:70
  84.1 9.7 %scatter_fusion = f32[64,128,256]{2,1,0:T(8,128)} fusion(f32[64,128,256]{2,1,0:T(8,128)} %get-tuple-element.263, s32[32]{0:T(128)S(1)} %get-tuple-element.243, f32[32,128,256]{2,1,0:T(8,128)} %fusion.44), kind=kCustom, calls=%fused_computation.2.clone.1 | custom fusion | flops 1048576 | bytes 12583040 | tf_op jit(solution)/shard_map/while/body/eval_jaxpr/scatter-add | solution.py:70
  102.4 9.7 %scatter_fusion = f32[64,128,256]{2,1,0:T(8,128)} fusion(f32[64,128,256]{2,1,0:T(8,128)} %get-tuple-element.263, s32[32]{0:T(128)S(1)} %get-tuple-element.243, f32[32,128,256]{2,1,0:T(8,128)} %fusion.44), kind=kCustom, calls=%fused_computation.2.clone.1 | custom fusion | flops 1048576 | bytes 12583040 | tf_op jit(solution)/shard_map/while/body/eval_jaxpr/scatter-add | solution.py:70
  120.7 9.7 %scatter_fusion = f32[64,128,256]{2,1,0:T(8,128)} fusion(f32[64,128,256]{2,1,0:T(8,128)} %get-tuple-element.263, s32[32]{0:T(128)S(1)} %get-tuple-element.243, f32[32,128,256]{2,1,0:T(8,128)} %fusion.44), kind=kCustom, calls=%fused_computation.2.clone.1 | custom fusion | flops 1048576 | bytes 12583040 | tf_op jit(solution)/shard_map/while/body/eval_jaxpr/scatter-add | solution.py:70
  139.0 9.7 %scatter_fusion = f32[64,128,256]{2,1,0:T(8,128)} fusion(f32[64,128,256]{2,1,0:T(8,128)} %get-tuple-element.263, s32[32]{0:T(128)S(1)} %get-tuple-element.243, f32[32,128,256]{2,1,0:T(8,128)} %fusion.44), kind=kCustom, calls=%fused_computation.2.clone.1 | custom fusion | flops 1048576 | bytes 12583040 | tf_op jit(solution)/shard_map/while/body/eval_jaxpr/scatter-add | solution.py:70
  157.2 9.8 %scatter_fusion = f32[64,128,256]{2,1,0:T(8,128)} fusion(f32[64,128,256]{2,1,0:T(8,128)} %get-tuple-element.263, s32[32]{0:T(128)S(1)} %get-tuple-element.243, f32[32,128,256]{2,1,0:T(8,128)} %fusion.44), kind=kCustom, calls=%fused_computation.2.clone.1 | custom fusion | flops 1048576 | bytes 12583040 | tf_op jit(solution)/shard_map/while/body/eval_jaxpr/scatter-add | solution.py:70
  175.6 9.8 %scatter_fusion = f32[64,128,256]{2,1,0:T(8,128)} fusion(f32[64,128,256]{2,1,0:T(8,128)} %get-tuple-element.263, s32[32]{0:T(128)S(1)} %get-tuple-element.243, f32[32,128,256]{2,1,0:T(8,128)} %fusion.44), kind=kCustom, calls=%fused_computation.2.clone.1 | custom fusion | flops 1048576 | bytes 12583040 | tf_op jit(solution)/shard_map/while/body/eval_jaxpr/scatter-add | solution.py:70
  194.0 10.0 %scatter_fusion = f32[64,128,256]{2,1,0:T(8,128)} fusion(f32[64,128,256]{2,1,0:T(8,128)} %get-tuple-element.263, s32[32]{0:T(128)S(1)} %get-tuple-element.243, f32[32,128,256]{2,1,0:T(8,128)} %fusion.44), kind=kCustom, calls=%fused_computation.2.clone.1 | custom fusion | flops 1048576 | bytes 12583040 | tf_op jit(solution)/shard_map/while/body/eval_jaxpr/scatter-add | solution.py:70
  205.2 119.9 %reduce-scatter.3.cloned.1.call-done = f32[512,256]{1,0:T(8,128)} async-done(((f32[8192,256]{1,0:T(8,128)}), f32[512,256]{1,0:T(8,128)}) %reduce-scatter.3.cloned.1.call-update) | async-done | bytes 524304 | tf_op jit(solution)/shard_map/reduce_scatter | solution.py:76
  330.5 120.3 %all-reduce.7.cloned.1.call-done = (f32[256,256]{0,1:T(8,128)}, f32[256,256]{0,1:T(8,128)}) async-done(((f32[256,256]{0,1:T(8,128)}, f32[256,256]{0,1:T(8,128)}), (f32[256,256]{0,1:T(8,128)}, f32[256,256]{0,1:T(8,128)})) %all-reduce.7.cloned.1.call-update) | async-done | bytes 524304 | tf_op jit(solution)/shard_map/psum | solution.py:16
  450.9 79.2 %all-gather.5.cloned.1.call-done = bf16[8192,256]{1,0:T(8,128)(2,1)} async-done(((bf16[512,256]{1,0:T(8,128)(2,1)}), bf16[8192,256]{1,0:T(8,128)(2,1)}) %all-gather.5.cloned.1.call-update) | async-done | bytes 4194320 | tf_op jit(solution)/shard_map/all_gather | solution.py:22
  534.4 150.1 %while.21 = (s32[]{:T(128)}, f32[64,128,256]{2,1,0:T(8,128)}, s32[8,32]{1,0:T(8,128)S(1)}, s32[8,4,32,128]{3,2,1,0:T(8,128)S(1)}, f32[8,32]{1,0:T(8,128)S(1)}, /...) while((s32[]{:T(128)}, f32[64,128,256]{2,1,0:T(8,128)}, s32[8,32]{1,0:T(8,128)S(1)}, ...), condition=%wide.region_8.9_spmd, body=%wide.region_5.8_spmd.sunk | while | flops 276300992 | bytes 27465064 | solution.py:34
  543.2 9.9 %scatter_fusion.1 = f32[64,128,256]{2,1,0:T(8,128)} fusion(f32[64,128,256]{2,1,0:T(8,128)} %get-tuple-element.287, s32[32]{0:T(128)S(1)} %get-tuple-element.252, f32[32,128,256]{2,1,0:T(8,128)} %fusion.48), kind=kCustom, calls=%fused_computation.3.clone.1 | custom fusion | flops 1048576 | bytes 12583040 | tf_op jit(solution)/shard_map/while/body/eval_jaxpr/scatter-add | solution.py:31
  561.8 10.1 %scatter_fusion.1 = f32[64,128,256]{2,1,0:T(8,128)} fusion(f32[64,128,256]{2,1,0:T(8,128)} %get-tuple-element.287, s32[32]{0:T(128)S(1)} %get-tuple-element.252, f32[32,128,256]{2,1,0:T(8,128)} %fusion.48), kind=kCustom, calls=%fused_computation.3.clone.1 | custom fusion | flops 1048576 | bytes 12583040 | tf_op jit(solution)/shard_map/while/body/eval_jaxpr/scatter-add | solution.py:31
  580.7 10.0 %scatter_fusion.1 = f32[64,128,256]{2,1,0:T(8,128)} fusion(f32[64,128,256]{2,1,0:T(8,128)} %get-tuple-element.287, s32[32]{0:T(128)S(1)} %get-tuple-element.252, f32[32,128,256]{2,1,0:T(8,128)} %fusion.48), kind=kCustom, calls=%fused_computation.3.clone.1 | custom fusion | flops 1048576 | bytes 12583040 | tf_op jit(solution)/shard_map/while/body/eval_jaxpr/scatter-add | solution.py:31
  599.4 10.1 %scatter_fusion.1 = f32[64,128,256]{2,1,0:T(8,128)} fusion(f32[64,128,256]{2,1,0:T(8,128)} %get-tuple-element.287, s32[32]{0:T(128)S(1)} %get-tuple-element.252, f32[32,128,256]{2,1,0:T(8,128)} %fusion.48), kind=kCustom, calls=%fused_computation.3.clone.1 | custom fusion | flops 1048576 | bytes 12583040 | tf_op jit(solution)/shard_map/while/body/eval_jaxpr/scatter-add | solution.py:31
  618.3 10.1 %scatter_fusion.1 = f32[64,128,256]{2,1,0:T(8,128)} fusion(f32[64,128,256]{2,1,0:T(8,128)} %get-tuple-element.287, s32[32]{0:T(128)S(1)} %get-tuple-element.252, f32[32,128,256]{2,1,0:T(8,128)} %fusion.48), kind=kCustom, calls=%fused_computation.3.clone.1 | custom fusion | flops 1048576 | bytes 12583040 | tf_op jit(solution)/shard_map/while/body/eval_jaxpr/scatter-add | solution.py:31
  637.1 10.1 %scatter_fusion.1 = f32[64,128,256]{2,1,0:T(8,128)} fusion(f32[64,128,256]{2,1,0:T(8,128)} %get-tuple-element.287, s32[32]{0:T(128)S(1)} %get-tuple-element.252, f32[32,128,256]{2,1,0:T(8,128)} %fusion.48), kind=kCustom, calls=%fused_computation.3.clone.1 | custom fusion | flops 1048576 | bytes 12583040 | tf_op jit(solution)/shard_map/while/body/eval_jaxpr/scatter-add | solution.py:31
  655.9 9.9 %scatter_fusion.1 = f32[64,128,256]{2,1,0:T(8,128)} fusion(f32[64,128,256]{2,1,0:T(8,128)} %get-tuple-element.287, s32[32]{0:T(128)S(1)} %get-tuple-element.252, f32[32,128,256]{2,1,0:T(8,128)} %fusion.48), kind=kCustom, calls=%fused_computation.3.clone.1 | custom fusion | flops 1048576 | bytes 12583040 | tf_op jit(solution)/shard_map/while/body/eval_jaxpr/scatter-add | solution.py:31
  674.6 9.9 %scatter_fusion.1 = f32[64,128,256]{2,1,0:T(8,128)} fusion(f32[64,128,256]{2,1,0:T(8,128)} %get-tuple-element.287, s32[32]{0:T(128)S(1)} %get-tuple-element.252, f32[32,128,256]{2,1,0:T(8,128)} %fusion.48), kind=kCustom, calls=%fused_computation.3.clone.1 | custom fusion | flops 1048576 | bytes 12583040 | tf_op jit(solution)/shard_map/while/body/eval_jaxpr/scatter-add | solution.py:31
  684.5 13.9 %all-reduce.5.cloned.1.call-done = (f32[256,256]{0,1:T(8,128)}, f32[256,256]{0,1:T(8,128)}) async-done(((f32[256,256]{0,1:T(8,128)}, f32[256,256]{0,1:T(8,128)}), (f32[256,256]{0,1:T(8,128)}, f32[256,256]{0,1:T(8,128)})) %all-reduce.5.cloned.1.call-update) | async-done | bytes 524304 | tf_op jit(solution)/shard_map/psum | solution.py:16
  701.2 99.0 %reduce-scatter.5.cloned.1.call-done = f32[512,256]{1,0:T(8,128)} async-done(((f32[8192,256]{1,0:T(8,128)}), f32[512,256]{1,0:T(8,128)}) %reduce-scatter.5.cloned.1.call-update) | async-done | bytes 524304 | tf_op jit(solution)/shard_map/reduce_scatter | solution.py:37
  (151 shorter events, 161.4 us)
Async XLA Ops:
  7.2 319.2 %copy-start = (bf16[256,256]{1,0:T(8,128)(2,1)S(1)}, bf16[256,256]{1,0:T(8,128)(2,1)}, u32[]{:S(2)}) copy-start(bf16[256,256]{1,0:T(8,128)(2,1)} %param.15) | copy-start | bytes 393220
  7.2 45.7 %all-gather.3.cloned.1.call-start = ((), (), s32[]{:S(2)}) async-start(), calls=%async_computation.2 | async-start | bytes 4456448 | tf_op jit(solution)/shard_map/all_gather | solution.py:61
  7.9 317.2 %reduce-scatter.3.cloned.1.call-start = ((), (), s32[]{:S(2)}) async-start(), calls=%async_computation.3 | async-start | bytes 8912896 | tf_op jit(solution)/shard_map/reduce_scatter | solution.py:76
  204.0 0.7 copy-start.3
  204.0 1.0 copy-start.1
  204.0 1.0 copy-start.2
  204.0 122.4 %copy-start.4 = (bf16[512,256]{1,0:T(8,128)(2,1)S(1)}, bf16[512,256]{1,0:T(8,128)(2,1)}, u32[]{:S(2)}) copy-start(bf16[512,256]{1,0:T(8,128)(2,1)} %param.16) | copy-start | bytes 786436
  204.0 246.8 %all-reduce.7.cloned.1.call-start = ((), (), s32[]{:S(2)}) async-start(), calls=%async_computation.7 | async-start | bytes 1048576 | tf_op jit(solution)/shard_map/psum | solution.py:16
  329.4 200.7 %all-gather.5.cloned.1.call-start = ((), (), s32[]{:S(2)}) async-start(), calls=%async_computation.4 | async-start | bytes 4456448 | tf_op jit(solution)/shard_map/all_gather | solution.py:22
  330.5 367.9 %all-reduce.5.cloned.1.call-start = ((), (), s32[]{:S(2)}) async-start(), calls=%async_computation.6 | async-start | bytes 1048576 | tf_op jit(solution)/shard_map/psum | solution.py:16
  450.9 349.3 %reduce-scatter.5.cloned.1.call-start = ((), (), s32[]{:S(2)}) async-start(), calls=%async_computation.5 | async-start | bytes 8912896 | tf_op jit(solution)/shard_map/reduce_scatter | solution.py:37
Sparse Core Ops, SparseCore 0:
  9.9 42.9 all-gather.2
  204.1 120.9 reduce-scatter.2
  329.6 121.2 all-reduce.6
  454.0 76.1 all-gather.4
  532.9 165.5 all-reduce.4
  700.8 99.2 reduce-scatter.4
